TPU v7x, 32 devices: a whole 2x2x4 slice. The times are simulated.
32 devices in a mesh: elem: 16 (over z, x, core), head: 2 (over y).
Axes of the slice: x: 2, y: 2, z: 4, core: 2. Of those that a mesh axis runs over, the one named last changes fastest.
Arguments:
- features: bfloat16 [16384, 512], P('elem'), may hold values from -6 to 6
- out_grad: bfloat16 [16384, 512], P('elem'), may hold values from -6 to 6
- bin_order: int32 [16384], P('elem'), may hold values from 0 to 16383, as said below
- key_lists: int32 [128, 12], P('elem'), may hold values from 0 to 127, as said below
- list_counts: int32 [128], P('elem'), may hold values from 1 to 12, as said below
- attn_gain: float32 [512], replicated, may hold values from 0.1 to 1.9
- query_weight: bfloat16 [512, 512], P(None, 'head')
- key_weight: bfloat16 [512, 512], P(None, 'head')
- value_weight: bfloat16 [512, 512], P(None, 'head'), may hold values from -0.25 to 0.25
- out_weight: bfloat16 [512, 512], P('head'), may hold values from -0.25 to 0.25
- ffn_gain: float32 [512], replicated, may hold values from 0.1 to 1.9
- ffn_in: bfloat16 [512, 2048], P(None, 'head'), may hold values from -0.25 to 0.25
- ffn_out: bfloat16 [2048, 512], P('head'), may hold values from -0.125 to 0.125
Outputs:
- output: bfloat16 [16384, 512], P('elem', 'head')
- input_grad: float32 [16384, 512], P('elem', 'head')
Inputs may be any that keep to these rules, and one draw needn't show every extreme that they name: `bin_order`: the rows of region e, numbers e * 1024 to (e + 1) * 1024 - 1, hold a permutation of those same numbers. `key_lists`: slot 0 of row b is b; the other slots hold distinct blocks other than b, all of the regions r - 1, r and r + 1 modulo 16, where r = b // 8 and region r holds blocks r * 8 to (r + 1) * 8 - 1; in row r * 8 of every region, slot 1 is a block of region r - 1 and slot 2 a block of region r + 1. list_counts[r * 8] = 12 for every region r.
All inputs are finite; a program needn't handle non-finite values.
Results may differ from a plain program's by a relative error of at most 0.024.
Values may be sent and summed in bfloat16 or wider, within the bound.
No kernel may reach another device: no remote copies, remote signals or barrier semaphores. Data moves between devices by JAX's collectives and lax.ppermute only.
A program may use at most 128 MiB of HBM per device.

v0:
```python
import jax
import jax.numpy as jnp
from jax import lax
from jax.sharding import PartitionSpec as P

HD = 64
EPSILON = 1e-05


def padded(block, sides, width):
    for axis, dim in sides:
        count = lax.axis_size(axis)
        forward = [(i, i + 1) for i in range(count - 1)]
        forward.append((count - 1, 0))
        backward = [(target, source) for source, target in forward]
        low = lax.ppermute(
            lax.slice_in_dim(block, block.shape[dim] - width, None, axis=dim), axis, forward
        )
        high = lax.ppermute(lax.slice_in_dim(block, 0, width, axis=dim), axis, backward)
        block = jnp.concatenate([low, block, high], axis=dim)
    return block


def from_behind(value, axis, steps):
    count = lax.axis_size(axis)
    pairs = [(source, (source + steps) % count) for source in range(count)]
    return lax.ppermute(value, axis, pairs)


def row_scale(values):
    return lax.rsqrt(jnp.mean(values * values, axis=-1, keepdims=True) + EPSILON)


def local(
    features,
    out_grad,
    bin_order,
    key_lists,
    list_counts,
    attn_gain,
    query_weight,
    key_weight,
    value_weight,
    out_weight,
    ffn_gain,
    ffn_in,
    ffn_out,
):
    row_count, model_width = features.shape
    block_count = key_lists.shape[0]
    block_len = row_count // block_count
    col_share = query_weight.shape[1]
    local_heads = col_share // HD
    scale_for_scores = HD ** (-0.5)
    highest_precision = lax.Precision.HIGHEST
    region = lax.axis_index("elem")
    regions = lax.axis_size("elem")
    head_group = lax.axis_index("head")
    col_start = head_group * col_share
    positions = bin_order - region * row_count
    owners = key_lists // block_count
    relative = jnp.mod(owners - region + 1, regions)
    buffer_index = relative * block_count + key_lists % block_count
    top_count = jnp.max(list_counts)
    wide_blocks = 3 * block_count
    block_ids = jnp.arange(wide_blocks, dtype=jnp.int32)
    ordered_rows = jnp.take(features, positions, axis=0).astype(jnp.float32)
    first_scale = row_scale(ordered_rows)
    first_norm = ordered_rows * first_scale
    normed = (first_norm * attn_gain).astype(jnp.bfloat16)
    queries = jnp.dot(normed, query_weight, preferred_element_type=jnp.float32).astype(jnp.bfloat16)
    pair_weights = jnp.concatenate([key_weight, value_weight], axis=1)
    widened = padded(normed, (("elem", 0),), row_count)
    pair_rows = jnp.dot(widened, pair_weights, preferred_element_type=jnp.float32).astype(
        jnp.bfloat16
    )
    wide_rows = 3 * row_count
    pair_blocks = pair_rows.reshape(wide_blocks, block_len, 2 * col_share)
    query_blocks = queries.reshape(block_count, block_len, local_heads, HD)

    def slot_table(slot_pos):
        picked = lax.dynamic_index_in_dim(buffer_index, slot_pos, axis=1, keepdims=False)
        return picked[:, None] == block_ids[None, :]

    def slot_scores(slot_pos):
        table = slot_table(slot_pos)
        tiles = jnp.einsum(
            "bc,ckf->bkf",
            table.astype(jnp.bfloat16),
            pair_blocks,
            preferred_element_type=jnp.float32,
        ).astype(jnp.bfloat16)
        key_tile_blocks = tiles[:, :, :col_share].reshape(block_count, block_len, local_heads, HD)
        value_tile_blocks = tiles[:, :, col_share:].reshape(block_count, block_len, local_heads, HD)
        attention_scores = (
            jnp.einsum(
                "bqhd,bkhd->bhqk", query_blocks, key_tile_blocks, preferred_element_type=jnp.float32
            )
            * scale_for_scores
        )
        live_mask = (slot_pos < list_counts)[:, None, None, None]
        return (
            jnp.where(live_mask, attention_scores, -jnp.inf),
            table,
            key_tile_blocks,
            value_tile_blocks,
        )

    first_scores, first_table, first_keys, first_values = slot_scores(0)
    run_max = jnp.max(first_scores, axis=-1)
    run_total = jnp.sum(jnp.exp(first_scores - run_max[..., None]), axis=-1)

    def stats_step(slot_pos, carried):
        old_max, old_total = carried
        attention_scores, table, key_tile_blocks, value_tile_blocks = slot_scores(slot_pos)
        new_max = jnp.maximum(old_max, jnp.max(attention_scores, axis=-1))
        new_total = old_total * jnp.exp(old_max - new_max) + jnp.sum(
            jnp.exp(attention_scores - new_max[..., None]), axis=-1
        )
        return (new_max, new_total)

    run_max, run_total = lax.fori_loop(1, top_count, stats_step, (run_max, run_total))
    log_total = run_max + jnp.log(run_total)

    def output_step(slot_pos, running):
        attention_scores, table, key_tile_blocks, value_tile_blocks = slot_scores(slot_pos)
        attn_probs = jnp.exp(attention_scores - log_total[..., None]).astype(jnp.bfloat16)
        return running + jnp.einsum(
            "bhqk,bkhd->bqhd", attn_probs, value_tile_blocks, preferred_element_type=jnp.float32
        )

    attended_sum = lax.fori_loop(
        0, top_count, output_step, jnp.zeros((block_count, block_len, local_heads, HD), jnp.float32)
    )
    attended_output = attended_sum.reshape(row_count, col_share).astype(jnp.bfloat16)
    mixed_heads = lax.psum(
        jnp.dot(attended_output, out_weight, preferred_element_type=jnp.float32).astype(
            jnp.bfloat16
        ),
        "head",
    ).astype(jnp.float32)
    hidden_in = ordered_rows + mixed_heads
    second_scale = row_scale(hidden_in)
    second_norm = hidden_in * second_scale
    normed_two = (second_norm * ffn_gain).astype(jnp.bfloat16)
    pre_act = jnp.dot(normed_two, ffn_in, preferred_element_type=jnp.float32)
    activated = jax.nn.gelu(pre_act).astype(jnp.bfloat16)
    ffn_terms = jnp.dot(activated, ffn_out, preferred_element_type=jnp.float32)
    ffn_total = lax.psum(ffn_terms.astype(jnp.bfloat16), "head").astype(jnp.float32)
    out_sorted = lax.dynamic_slice_in_dim(hidden_in + ffn_total, col_start, col_share, 1).astype(
        jnp.bfloat16
    )
    grad_sorted = jnp.take(out_grad, positions, axis=0)
    grad_act = jnp.dot(grad_sorted, ffn_out.T, preferred_element_type=jnp.float32)
    gelu_value, gelu_pull = jax.vjp(jax.nn.gelu, pre_act)
    grad_pre = gelu_pull(grad_act)[0].astype(jnp.bfloat16)
    norm_grad = lax.psum(
        jnp.dot(grad_pre, ffn_in.T, preferred_element_type=jnp.float32).astype(jnp.bfloat16), "head"
    ).astype(jnp.float32)
    scaled_grad = norm_grad * ffn_gain
    grad_hidden = grad_sorted.astype(jnp.float32) + second_scale * (
        scaled_grad - second_norm * jnp.mean(scaled_grad * second_norm, axis=-1, keepdims=True)
    )
    grad_mixed = jnp.dot(
        grad_hidden.astype(jnp.bfloat16), out_weight.T, preferred_element_type=jnp.float32
    ).astype(jnp.bfloat16)
    output = jnp.zeros_like(out_sorted).at[positions].set(out_sorted)
    grad_blocks = grad_mixed.reshape(block_count, block_len, local_heads, HD)
    attended_blocks = attended_output.reshape(block_count, block_len, local_heads, HD)
    deltas = jnp.einsum(
        "bqhd,bqhd->bhq", grad_blocks, attended_blocks, preferred_element_type=jnp.float32
    )

    def back_step(slot_pos, carried):
        query_gradient, grad_pair_blocks = carried
        attention_scores, table, key_tile_blocks, value_tile_blocks = slot_scores(slot_pos)
        complete_probabilities = jnp.exp(attention_scores - log_total[..., None])
        probability_gradient = jnp.einsum(
            "bqhd,bkhd->bhqk", grad_blocks, value_tile_blocks, preferred_element_type=jnp.float32
        )
        score_gradient = (
            complete_probabilities * (probability_gradient - deltas[..., None])
        ).astype(jnp.bfloat16)
        query_gradient = (
            query_gradient
            + jnp.einsum(
                "bhqk,bkhd->bqhd",
                score_gradient,
                key_tile_blocks,
                preferred_element_type=jnp.float32,
            )
            * scale_for_scores
        )
        key_portion = (
            jnp.einsum(
                "bhqk,bqhd->bkhd", score_gradient, query_blocks, preferred_element_type=jnp.float32
            )
            * scale_for_scores
        )
        value_portion = jnp.einsum(
            "bhqk,bqhd->bkhd",
            complete_probabilities.astype(jnp.bfloat16),
            grad_blocks,
            preferred_element_type=jnp.float32,
        )
        portion = jnp.concatenate(
            [
                key_portion.reshape(block_count, block_len, col_share),
                value_portion.reshape(block_count, block_len, col_share),
            ],
            axis=2,
        )
        grad_pair_blocks = grad_pair_blocks + jnp.einsum(
            "bc,bkf->ckf", table.astype(jnp.float32), portion, precision=highest_precision
        )
        return (query_gradient, grad_pair_blocks)

    zero_query = jnp.zeros((block_count, block_len, local_heads, HD), jnp.float32)
    zero_wide = jnp.zeros((wide_blocks, block_len, 2 * col_share), jnp.float32)
    query_gradient, grad_pair_blocks = lax.fori_loop(
        0, top_count, back_step, (zero_query, zero_wide)
    )
    grad_pairs = grad_pair_blocks.reshape(wide_rows, 2 * col_share)
    pair_wide = pair_weights.astype(jnp.float32)
    query_part = jnp.dot(
        query_gradient.reshape(row_count, col_share),
        query_weight.astype(jnp.float32).T,
        precision=highest_precision,
    )
    grad_wide = jnp.dot(grad_pairs, pair_wide.T, precision=highest_precision)
    from_right = from_behind(grad_wide[:row_count].astype(jnp.bfloat16), "elem", -1).astype(
        jnp.float32
    )
    from_left = from_behind(grad_wide[2 * row_count :].astype(jnp.bfloat16), "elem", 1).astype(
        jnp.float32
    )
    group_term = query_part + grad_wide[row_count : 2 * row_count] + from_right + from_left
    grad_norm = lax.psum(group_term.astype(jnp.bfloat16), "head").astype(jnp.float32)
    scaled_one = grad_norm * attn_gain
    row_gradients = grad_hidden + first_scale * (
        scaled_one - first_norm * jnp.mean(scaled_one * first_norm, axis=-1, keepdims=True)
    )
    grad_share = lax.dynamic_slice_in_dim(row_gradients, col_start, col_share, 1)
    input_grad = jnp.zeros_like(grad_share).at[positions].set(grad_share)
    return (output, input_grad)


def solution(mesh):
    in_specs = (
        P("elem", None),
        P("elem", None),
        P("elem"),
        P("elem", None),
        P("elem"),
        P(),
        P(None, "head"),
        P(None, "head"),
        P(None, "head"),
        P("head", None),
        P(),
        P(None, "head"),
        P("head", None),
    )
    out_specs = (P("elem", "head"), P("elem", "head"))
    return jax.shard_map(local, mesh=mesh, in_specs=in_specs, out_specs=out_specs, check_vma=False)
```

profile of v0, /device:TPU:0, one launch (start us, length us, event | category | flops | bytes accessed | tf_op | source)
XLA Modules:
  0.0 722.0 jit_solution(11235072406354910245)
XLA Ops:
  8.6 5.4 gather_fusion
  15.2 5.4 collective-permute-start.1
  28.5 4.4 collective-permute-done.1
  32.9 4.8 collective-permute-done
  48.6 56.0 %while.37 = (s32[]{:T(128)}, f32[8,4,128]{2,1,0:T(4,128)S(1)}, f32[8,4,128]{2,1,0:T(4,128)S(1)}, s32[]{:T(128)}, s32[8]{0:T(128)S(1)}, /*index=5*/s32[8,12]{0,1:...) while((s32[]{:T(128)}, f32[8,4,128]{2,1,0:T(4,128)S(1)}, ...), condition=%wide.region_7.9_spmd.clone, body=%wide.region_4.8_spmd.clone.sunk | while | flops 95953104 | bytes 11747639 | solution.py:122
  105.8 95.0 %while.38 = (s32[]{:T(128)}, f32[8,128,4,64]{1,3,2,0:T(8,128)}, s32[]{:T(128)}, s32[8,12]{0,1:T(8,128)S(1)}, bf16[24,128,512]{2,0,1:T(8,128)(2,1)}, /*index=5*/s...) while((s32[]{:T(128)}, f32[8,128,4,64]{1,3,2,0:T(8,128)}, ...), condition=%wide.region_9.11_spmd.clone, body=%wide.region_8.10_spmd.clone.sunk | while | flops 162267344 | bytes 12075311 | solution.py:132
  110.0 3.7 fusion.180
  204.1 5.1 gather_fusion.1
  209.1 40.8 %all-reduce.5.cloned.1.call-done = bf16[1024,512]{1,0:T(8,128)(2,1)} async-done(((bf16[1024,512]{1,0:T(8,128)(2,1)}), bf16[1024,512]{1,0:T(8,128)(2,1)}) %all-reduce.5.cloned.1.call-update) | async-done | bytes 1048592 | tf_op jit(solution)/shard_map/psum | solution.py:136
  255.6 7.6 %fusion.58 = bf16[1024,512]{1,0:T(8,128)(2,1)} fusion(bf16[512,1024]{1,0:T(8,128)(2,1)S(1)} %copy-done, f32[1024,1024]{1,0:T(8,128)} %fusion.60, bf16[1024,512]{1,0:T(8,128)(2,1)} %param.33, bf16[1024,512]{1,0:T(8,128)(2,1)} %gather_fusion.1, pred[1024]{0:T(1024)(128)(4,1)S(1)} %get-tuple-element.344), kind=kOutput, calls=%fused_computation.94 | convolution fusion | flops 2169503744 | bytes 8389632 | tf_op jit(solution)/shard_map/dot_general | solution.py:158
  263.4 39.9 %all-reduce.7.cloned.1.call-done = bf16[1024,512]{1,0:T(8,128)(2,1)} async-done(((bf16[1024,512]{1,0:T(8,128)(2,1)}), bf16[1024,512]{1,0:T(8,128)(2,1)}) %all-reduce.7.cloned.1.call-update) | async-done | bytes 1048592 | tf_op jit(solution)/shard_map/psum | solution.py:157
  314.5 279.4 %while.39 = (s32[]{:T(128)}, f32[8,128,4,64]{1,3,2,0:T(8,128)}, f32[24,128,512]{2,0,1:T(8,128)}, s32[]{:T(128)}, s32[8,12]{0,1:T(8,128)S(1)}, /*index=5*/bf16[24...) while((s32[]{:T(128)}, f32[8,128,4,64]{1,3,2,0:T(8,128)}, ...), condition=%wide.region_17.19_spmd.clone, body=%wide.region_16.18_spmd.clone.sunk | while | flops 518783360 | bytes 61374988 | solution.py:220
  331.0 6.7 convolution_add_fusion.2
  354.2 6.7 convolution_add_fusion.2
  377.4 6.7 convolution_add_fusion.2
  400.6 6.7 convolution_add_fusion.2
  423.8 6.7 convolution_add_fusion.2
  447.0 6.7 convolution_add_fusion.2
  470.2 6.7 convolution_add_fusion.2
  493.4 6.7 convolution_add_fusion.2
  516.6 6.7 convolution_add_fusion.2
  539.8 6.7 convolution_add_fusion.2
  563.0 6.7 convolution_add_fusion.2
  586.2 6.7 convolution_add_fusion.2
  593.9 6.5 copy.60
  600.4 5.5 fusion.108
  606.2 4.6 collective-permute-start.2
  613.8 9.3 %collective-permute-done.3 = bf16[1024,512]{1,0:T(8,128)(2,1)S(1)} collective-permute-done((bf16[1024,512]{1,0:T(8,128)(2,1)S(1)}, bf16[1024,512]{1,0:T(8,128)(2,1)S(1)}, u32[]{:S(2)}, u32[]{:S(2)}) %collective-permute-start.3) | collective-permute-done | bytes 1048608 | tf_op jit(solution)/shard_map/ppermute | solution.py:27
  626.2 71.7 %all-reduce.9.cloned.1.call-done = (bf16[1024,512]{1,0:T(8,128)(2,1)}, bf16[1024,512]{1,0:T(8,128)(2,1)}) async-done(((bf16[1024,512]{1,0:T(8,128)(2,1)}, bf16[1024,512]{1,0:T(8,128)(2,1)}), (bf16[1024,512]{1,0:T(8,128)(2,1)}, bf16[1024,512]{1,0:T(8,128)(2,1)})) %all-reduce.9.cloned.1.call-update) | async-done | bytes 2097168 | tf_op jit(solution)/shard_map/psum | solution.py:149
  697.9 4.0 multiply_reduce_fusion
  701.9 6.1 scatter_custom_fusion
  708.1 7.2 scatter_custom_fusion.1
  (608 shorter events, 367.8 us)
Async XLA Ops:
  7.2 245.0 %copy-start = (bf16[512,1024]{1,0:T(8,128)(2,1)S(1)}, bf16[512,1024]{1,0:T(8,128)(2,1)}, u32[]{:S(2)}) copy-start(bf16[512,1024]{1,0:T(8,128)(2,1)} %param.32) | copy-start | bytes 3145732
  7.2 242.8 %all-reduce.5.cloned.1.call-start = ((), (), s32[]{:S(2)}) async-start(), calls=%async_computation | async-start | bytes 2097152 | tf_op jit(solution)/shard_map/psum | solution.py:136
  8.6 6.0 copy-start.30
  14.0 7.9 %copy-start.13 = (bf16[1024,512]{1,0:T(8,128)(2,1)}, bf16[1024,512]{1,0:T(8,128)(2,1)S(1)}, u32[]{:S(2)}) copy-start(bf16[1024,512]{1,0:T(8,128)(2,1)S(1)} %gather_fusion) | copy-start | bytes 3145732
  14.0 6.6 copy-start.22
  15.2 17.7 %collective-permute-start.1 = (bf16[1024,512]{1,0:T(8,128)(2,1)S(1)}, bf16[1024,512]{1,0:T(8,128)(2,1)}, u32[]{:S(2)}, u32[]{:S(2)}) collective-permute-start(bf16[1024,512]{1,0:T(8,128)(2,1)S(1)} %multiply_convert_fusion.3), channel_id=1, source_target_pairs={{2,0},{4,2},{6,4},{8,6},{10,8},{12,10},{14,12},{16,14},{18,16},{20... | collective-permute-start | bytes 3145736 | tf_op jit(solution)/shard_map/ppermute | solution.py:19
  20.6 17.1 %collective-permute-start = (bf16[1024,512]{1,0:T(8,128)(2,1)S(1)}, bf16[1024,512]{1,0:T(8,128)(2,1)}, u32[]{:S(2)}, u32[]{:S(2)}) collective-permute-start(bf16[1024,512]{1,0:T(8,128)(2,1)S(1)} %multiply_convert_fusion.3), channel_id=1, source_target_pairs={{0,2},{2,4},{4,6},{6,8},{8,10},{10,12},{12,14},{14,16},{16,18},{18... | collective-permute-start | bytes 3145736 | tf_op jit(solution)/shard_map/ppermute | solution.py:16
  23.9 3.6 copy-start.25
  28.5 12.6 %copy-start.20 = (bf16[512,512]{1,0:T(8,128)(2,1)}, bf16[512,512]{1,0:T(8,128)(2,1)S(1)}, u32[]{:S(2)}) copy-start(bf16[512,512]{1,0:T(8,128)(2,1)S(1)} %constant_dynamic-update-slice_fusion) | copy-start | bytes 1572868
  204.0 99.3 %all-reduce.7.cloned.1.call-start = ((), (), s32[]{:S(2)}) async-start(), calls=%async_computation.1 | async-start | bytes 2097152 | tf_op jit(solution)/shard_map/psum | solution.py:157
  209.1 43.1 %copy-start.28 = (f32[512]{0:T(512)S(1)}, f32[512]{0:T(512)}, u32[]{:S(2)}) copy-start(f32[512]{0:T(512)} %param.31) | copy-start | bytes 6148
  252.2 53.0 %copy-start.7 = (f32[1024,512]{1,0:T(8,128)}, f32[1024,512]{1,0:T(8,128)S(1)}, u32[]{:S(2)}) copy-start(f32[1024,512]{1,0:T(8,128)S(1)} %get-tuple-element.343) | copy-start | bytes 6291460
  263.1 42.1 %copy-start.18 = (bf16[1024,512]{1,0:T(8,128)(2,1)S(1)}, bf16[1024,512]{1,0:T(8,128)(2,1)}, u32[]{:S(2)}) copy-start(bf16[1024,512]{1,0:T(8,128)(2,1)} %gather_fusion.1) | copy-start | bytes 3145732
  263.1 434.8 %all-reduce.9.cloned.1.call-start = ((), (), s32[]{:S(2)}) async-start(), calls=%async_computation.2 | async-start | bytes 4194304 | tf_op jit(solution)/shard_map/psum | solution.py:149
  319.0 3.2 copy-start.5
  342.2 3.2 copy-start.5
  365.4 3.2 copy-start.5
  388.6 3.2 copy-start.5
  411.8 3.2 copy-start.5
  435.0 3.2 copy-start.5
  593.9 6.5 copy-start.21
  600.4 10.3 %copy-start.33 = (bf16[1024,512]{1,0:T(8,128)(2,1)S(1)}, bf16[1024,512]{1,0:T(8,128)(2,1)}, u32[]{:S(2)}) copy-start(bf16[1024,512]{1,0:T(8,128)(2,1)} %param.33) | copy-start | bytes 3145732
  605.9 4.8 copy-start.16
  606.1 17.1 %collective-permute-start.3 = (bf16[1024,512]{1,0:T(8,128)(2,1)S(1)}, bf16[1024,512]{1,0:T(8,128)(2,1)S(1)}, u32[]{:S(2)}, u32[]{:S(2)}) collective-permute-start(bf16[1024,512]{1,0:T(8,128)(2,1)S(1)} %get-tuple-element.353), channel_id=1, source_target_pairs={{0,2},{2,4},{4,6},{6,8},{8,10},{10,12},{12,14},{14,16},{16,18},{18... | collective-permute-start | bytes 3145736 | tf_op jit(solution)/shard_map/ppermute | solution.py:27
  606.1 7.1 copy-start.12
  606.2 17.0 %collective-permute-start.2 = (bf16[1024,512]{1,0:T(8,128)(2,1)S(1)}, bf16[1024,512]{1,0:T(8,128)(2,1)S(1)}, u32[]{:S(2)}, u32[]{:S(2)}) collective-permute-start(bf16[1024,512]{1,0:T(8,128)(2,1)S(1)} %get-tuple-element.352), channel_id=1, source_target_pairs={{0,30},{2,0},{4,2},{6,4},{8,6},{10,8},{12,10},{14,12},{16,14},{18,... | collective-permute-start | bytes 3145736 | tf_op jit(solution)/shard_map/ppermute | solution.py:27
  613.2 10.0 %copy-start.23 = (bf16[512,256]{1,0:T(8,128)(2,1)S(1)}, bf16[512,256]{1,0:T(8,128)(2,1)}, u32[]{:S(2)}) copy-start(bf16[512,256]{1,0:T(8,128)(2,1)} %param.27) | copy-start | bytes 786436
  626.2 71.7 %copy-start.14 = (bf16[1024,512]{1,0:T(8,128)(2,1)S(1)}, bf16[1024,512]{1,0:T(8,128)(2,1)}, u32[]{:S(2)}) copy-start(bf16[1024,512]{1,0:T(8,128)(2,1)} %copy-done.13) | copy-start | bytes 3145732
  626.2 71.7 %copy-start.27 = (f32[1024]{0:T(1024)S(1)}, f32[1024]{0:T(1024)}, u32[]{:S(2)}) copy-start(f32[1024]{0:T(1024)} %copy-done.26) | copy-start | bytes 12292
  626.2 71.7 %copy-start.31 = (f32[512]{0:T(512)S(1)}, f32[512]{0:T(512)}, u32[]{:S(2)}) copy-start(f32[512]{0:T(512)} %param.26) | copy-start | bytes 6148
  697.9 4.0 copy-start.8
  708.1 7.2 copy-start.1
  (76 other events, 150.3 us)
Sparse Core Ops, SparseCore 0:
  204.1 45.7 all-reduce.4
  263.3 40.0 all-reduce.6
  626.4 71.5 all-reduce.8
where the time goes:
time: 734 us; the launch traced here: 722 us
  matrix products  348 us (47%)
  waiting for transfers between devices  171 us (23%)
  local copies, waits for them, and re-layouts  117 us (16%)
  other arithmetic  33.7 us (5%)
  loops' own time  27.3 us (4%)
  between operations  14.4 us (2%)
  starting transfers between devices  10.4 us (1%)
    dot_general x36, matrix products, slot_scores(): jnp.einsum('bc,ckf->bkf', table.astype(jnp.bfloat16), pair_blocks, prefer...  91.6 us
    dot_general x12, matrix products, back_step(): jnp.einsum('bc,bkf->ckf', table.astype(jnp.float32), portion, precision=h...  80.6 us
    psum x1, waiting for transfers between devices, local(): lax.psum(ffn_terms.astype(jnp.bfloat16), 'head').astype(jnp.float32)  71.7 us
    dot_general x12, matrix products, output_step(): jnp.einsum('bhqk,bkhd->bqhd', attn_probs, value_tile_blocks, preferred_el...  44.3 us
    psum x1, waiting for transfers between devices, local(): lax.psum(jnp.dot(attended_output, out_weight, preferred_element_type=jnp....  40.8 us
    psum x1, waiting for transfers between devices, local(): lax.psum(jnp.dot(grad_pre, ffn_in.T, preferred_element_type=jnp.float32)....  39.9 us
    dot_general x24, matrix products, slot_scores(): jnp.einsum('bqhd,bkhd->bhqk', query_blocks, key_tile_blocks, preferred_el...  32.1 us
    slice x36, local copies, waits for them, and re-layouts, slot_scores(): tiles[:, :, col_share:].reshape(block_count, block_len, local_heads, HD)  29.8 us
  transfers between devices with their start and end apart: 7, of which 6 were waited for; matrix products, arithmetic and copies ran while one was open for 2% of the time, Pallas kernels for 0%

commit v1 on v0

--- a/solution.py
+++ b/solution.py
@@ -2,9 +2,14 @@
 import jax.numpy as jnp
 from jax import lax
 from jax.sharding import PartitionSpec as P
+from jax.lax import all_gather
 
 HD = 64
 EPSILON = 1e-05
+
+
+def list_inputs_over_axis(local_values):
+    return all_gather(local_values, "head").sum(axis=0)
 
 
 def padded(block, sides, width):
@@ -133,11 +138,10 @@
         0, top_count, output_step, jnp.zeros((block_count, block_len, local_heads, HD), jnp.float32)
     )
     attended_output = attended_sum.reshape(row_count, col_share).astype(jnp.bfloat16)
-    mixed_heads = lax.psum(
+    mixed_heads = list_inputs_over_axis(
         jnp.dot(attended_output, out_weight, preferred_element_type=jnp.float32).astype(
             jnp.bfloat16
-        ),
-        "head",
+        )
     ).astype(jnp.float32)
     hidden_in = ordered_rows + mixed_heads
     second_scale = row_scale(hidden_in)

time: 734 us -> 731 us (level)
    psum x1 -> x0, waiting for transfers between devices: 40.8 us -> none  [local(): lax.psum(jnp.dot(attended_output, out_weight, preferred_element_type=jnp....]
    all_gather x0 -> x1, waiting for transfers between devices: none -> 33.7 us  [list_inputs_over_axis(): return all_gather(local_values, 'head').sum(axis=0)]
where the time goes in v1:
time: 731 us; the launch traced here: 719 us
  matrix products  348 us (48%)
  waiting for transfers between devices  164 us (22%)
  local copies, waits for them, and re-layouts  117 us (16%)
  other arithmetic  37 us (5%)
  loops' own time  27.7 us (4%)
  between operations  14.7 us (2%)
  starting transfers between devices  10.5 us (1%)
    dot_general x36, matrix products, slot_scores(): jnp.einsum('bc,ckf->bkf', table.astype(jnp.bfloat16), pair_blocks, prefer...  91.6 us
    dot_general x12, matrix products, back_step(): jnp.einsum('bc,bkf->ckf', table.astype(jnp.float32), portion, precision=h...  80.6 us
    psum x1, waiting for transfers between devices, local(): lax.psum(ffn_terms.astype(jnp.bfloat16), 'head').astype(jnp.float32)  71.7 us
    dot_general x12, matrix products, output_step(): jnp.einsum('bhqk,bkhd->bqhd', attn_probs, value_tile_blocks, preferred_el...  44.3 us
    psum x1, waiting for transfers between devices, local(): lax.psum(jnp.dot(grad_pre, ffn_in.T, preferred_element_type=jnp.float32)....  40.2 us
    all_gather x1, waiting for transfers between devices, list_inputs_over_axis(): return all_gather(local_values, 'head').sum(axis=0)  33.7 us
    dot_general x24, matrix products, slot_scores(): jnp.einsum('bqhd,bkhd->bhqk', query_blocks, key_tile_blocks, preferred_el...  32.1 us
    slice x36, local copies, waits for them, and re-layouts, slot_scores(): tiles[:, :, col_share:].reshape(block_count, block_len, local_heads, HD)  29.8 us
  transfers between devices with their start and end apart: 7, of which 6 were waited for; matrix products, arithmetic and copies ran while one was open for 2% of the time, Pallas kernels for 0%

profile of v1, /device:TPU:0, one launch (start us, length us, event | category | flops | bytes accessed | tf_op | source)
XLA Modules:
  0.0 719.1 jit_solution(14757700686750057754)
XLA Ops:
  8.6 5.4 gather_fusion
  15.2 5.4 collective-permute-start.1
  28.5 4.4 collective-permute-done.1
  32.9 4.8 collective-permute-done
  48.6 56.4 %while.37 = (s32[]{:T(128)}, f32[8,4,128]{2,1,0:T(4,128)S(1)}, f32[8,4,128]{2,1,0:T(4,128)S(1)}, s32[]{:T(128)}, s32[8]{0:T(128)S(1)}, /*index=5*/s32[8,12]{0,1:...) while((s32[]{:T(128)}, f32[8,4,128]{2,1,0:T(4,128)S(1)}, ...), condition=%wide.region_7.9_spmd.clone, body=%wide.region_4.8_spmd.clone.sunk | while | flops 95953104 | bytes 11747639 | solution.py:127
  106.1 95.0 %while.38 = (s32[]{:T(128)}, f32[8,128,4,64]{1,3,2,0:T(8,128)}, s32[]{:T(128)}, s32[8,12]{0,1:T(8,128)S(1)}, bf16[24,128,512]{2,0,1:T(8,128)(2,1)}, /*index=5*/s...) while((s32[]{:T(128)}, f32[8,128,4,64]{1,3,2,0:T(8,128)}, ...), condition=%wide.region_9.11_spmd.clone, body=%wide.region_8.10_spmd.clone.sunk | while | flops 162267344 | bytes 12075311 | solution.py:137
  110.3 3.7 fusion.180
  204.6 5.1 gather_fusion.1
  209.7 33.7 %all-gather.3.cloned.1.call-done = bf16[2048,512]{1,0:T(8,128)(2,1)} async-done(((bf16[1024,512]{1,0:T(8,128)(2,1)}), bf16[2048,512]{1,0:T(8,128)(2,1)}) %all-gather.3.cloned.1.call-update) | async-done | bytes 2097168 | tf_op jit(solution)/shard_map/all_gather | solution.py:12
  252.2 7.6 %fusion.58 = bf16[1024,512]{1,0:T(8,128)(2,1)} fusion(bf16[512,1024]{1,0:T(8,128)(2,1)S(1)} %copy-done, f32[1024,1024]{1,0:T(8,128)} %fusion.60, bf16[1024,512]{1,0:T(8,128)(2,1)} %param.33, bf16[1024,512]{1,0:T(8,128)(2,1)} %gather_fusion.1, pred[1024]{0:T(1024)(128)(4,1)S(1)} %get-tuple-element.344), kind=kOutput, calls=%fused_computation.94 | convolution fusion | flops 2169503744 | bytes 8389632 | tf_op jit(solution)/shard_map/dot_general | solution.py:162
  259.9 40.2 %all-reduce.4.cloned.1.call-done = bf16[1024,512]{1,0:T(8,128)(2,1)} async-done(((bf16[1024,512]{1,0:T(8,128)(2,1)}), bf16[1024,512]{1,0:T(8,128)(2,1)}) %all-reduce.4.cloned.1.call-update) | async-done | bytes 1048592 | tf_op jit(solution)/shard_map/psum | solution.py:161
  311.2 279.5 %while.39 = (s32[]{:T(128)}, f32[8,128,4,64]{1,3,2,0:T(8,128)}, f32[24,128,512]{2,0,1:T(8,128)}, s32[]{:T(128)}, s32[8,12]{0,1:T(8,128)S(1)}, /*index=5*/bf16[24...) while((s32[]{:T(128)}, f32[8,128,4,64]{1,3,2,0:T(8,128)}, ...), condition=%wide.region_17.19_spmd.clone, body=%wide.region_16.18_spmd.clone.sunk | while | flops 518783360 | bytes 61374988 | solution.py:224
  327.9 6.7 convolution_add_fusion.2
  351.1 6.7 convolution_add_fusion.2
  374.3 6.7 convolution_add_fusion.2
  397.5 6.7 convolution_add_fusion.2
  420.7 6.7 convolution_add_fusion.2
  443.9 6.7 convolution_add_fusion.2
  467.1 6.7 convolution_add_fusion.2
  490.3 6.7 convolution_add_fusion.2
  513.5 6.7 convolution_add_fusion.2
  536.7 6.7 convolution_add_fusion.2
  559.9 6.7 convolution_add_fusion.2
  583.1 6.7 convolution_add_fusion.2
  590.7 6.5 copy.60
  597.2 5.5 fusion.108
  602.9 4.7 collective-permute-start.2
  610.7 9.2 %collective-permute-done.3 = bf16[1024,512]{1,0:T(8,128)(2,1)S(1)} collective-permute-done((bf16[1024,512]{1,0:T(8,128)(2,1)S(1)}, bf16[1024,512]{1,0:T(8,128)(2,1)S(1)}, u32[]{:S(2)}, u32[]{:S(2)}) %collective-permute-start.3) | collective-permute-done | bytes 1048608 | tf_op jit(solution)/shard_map/ppermute | solution.py:32
  623.0 71.7 %all-reduce.6.cloned.1.call-done = (bf16[1024,512]{1,0:T(8,128)(2,1)}, bf16[1024,512]{1,0:T(8,128)(2,1)}) async-done(((bf16[1024,512]{1,0:T(8,128)(2,1)}, bf16[1024,512]{1,0:T(8,128)(2,1)}), (bf16[1024,512]{1,0:T(8,128)(2,1)}, bf16[1024,512]{1,0:T(8,128)(2,1)})) %all-reduce.6.cloned.1.call-update) | async-done | bytes 2097168 | tf_op jit(solution)/shard_map/psum | solution.py:153
  694.7 4.0 multiply_reduce_fusion
  698.7 6.1 scatter_custom_fusion
  704.9 7.2 scatter_custom_fusion.1
  (609 shorter events, 371.1 us)
Async XLA Ops:
  7.2 241.7 %copy-start = (bf16[512,1024]{1,0:T(8,128)(2,1)S(1)}, bf16[512,1024]{1,0:T(8,128)(2,1)}, u32[]{:S(2)}) copy-start(bf16[512,1024]{1,0:T(8,128)(2,1)} %param.32) | copy-start | bytes 3145732
  7.2 236.2 %all-gather.3.cloned.1.call-start = ((), (), s32[]{:S(2)}) async-start(), calls=%async_computation.1 | async-start | bytes 3145728 | tf_op jit(solution)/shard_map/all_gather | solution.py:12
  8.6 6.0 copy-start.30
  14.0 7.9 %copy-start.13 = (bf16[1024,512]{1,0:T(8,128)(2,1)}, bf16[1024,512]{1,0:T(8,128)(2,1)S(1)}, u32[]{:S(2)}) copy-start(bf16[1024,512]{1,0:T(8,128)(2,1)S(1)} %gather_fusion) | copy-start | bytes 3145732
  14.0 6.6 copy-start.22
  15.2 17.7 %collective-permute-start.1 = (bf16[1024,512]{1,0:T(8,128)(2,1)S(1)}, bf16[1024,512]{1,0:T(8,128)(2,1)}, u32[]{:S(2)}, u32[]{:S(2)}) collective-permute-start(bf16[1024,512]{1,0:T(8,128)(2,1)S(1)} %multiply_convert_fusion.3), channel_id=1, source_target_pairs={{2,0},{4,2},{6,4},{8,6},{10,8},{12,10},{14,12},{16,14},{18,16},{20... | collective-permute-start | bytes 3145736 | tf_op jit(solution)/shard_map/ppermute | solution.py:24
  20.6 17.1 %collective-permute-start = (bf16[1024,512]{1,0:T(8,128)(2,1)S(1)}, bf16[1024,512]{1,0:T(8,128)(2,1)}, u32[]{:S(2)}, u32[]{:S(2)}) collective-permute-start(bf16[1024,512]{1,0:T(8,128)(2,1)S(1)} %multiply_convert_fusion.3), channel_id=1, source_target_pairs={{0,2},{2,4},{4,6},{6,8},{8,10},{10,12},{12,14},{14,16},{16,18},{18... | collective-permute-start | bytes 3145736 | tf_op jit(solution)/shard_map/ppermute | solution.py:21
  23.9 3.6 copy-start.25
  28.5 12.6 %copy-start.20 = (bf16[512,512]{1,0:T(8,128)(2,1)}, bf16[512,512]{1,0:T(8,128)(2,1)S(1)}, u32[]{:S(2)}) copy-start(bf16[512,512]{1,0:T(8,128)(2,1)S(1)} %constant_dynamic-update-slice_fusion) | copy-start | bytes 1572868
  204.4 95.7 %all-reduce.4.cloned.1.call-start = ((), (), s32[]{:S(2)}) async-start(), calls=%async_computation | async-start | bytes 2097152 | tf_op jit(solution)/shard_map/psum | solution.py:161
  248.9 53.0 %copy-start.7 = (f32[1024,512]{1,0:T(8,128)}, f32[1024,512]{1,0:T(8,128)S(1)}, u32[]{:S(2)}) copy-start(f32[1024,512]{1,0:T(8,128)S(1)} %get-tuple-element.343) | copy-start | bytes 6291460
  259.8 42.1 %copy-start.18 = (bf16[1024,512]{1,0:T(8,128)(2,1)S(1)}, bf16[1024,512]{1,0:T(8,128)(2,1)}, u32[]{:S(2)}) copy-start(bf16[1024,512]{1,0:T(8,128)(2,1)} %gather_fusion.1) | copy-start | bytes 3145732
  259.8 434.9 %all-reduce.6.cloned.1.call-start = ((), (), s32[]{:S(2)}) async-start(), calls=%async_computation.2 | async-start | bytes 4194304 | tf_op jit(solution)/shard_map/psum | solution.py:153
  315.9 3.2 copy-start.5
  339.1 3.2 copy-start.5
  362.3 3.2 copy-start.5
  385.5 3.2 copy-start.5
  408.7 3.2 copy-start.5
  431.9 3.2 copy-start.5
  455.1 3.2 copy-start.5
  590.7 6.5 copy-start.21
  597.2 10.4 %copy-start.33 = (bf16[1024,512]{1,0:T(8,128)(2,1)S(1)}, bf16[1024,512]{1,0:T(8,128)(2,1)}, u32[]{:S(2)}) copy-start(bf16[1024,512]{1,0:T(8,128)(2,1)} %param.33) | copy-start | bytes 3145732
  602.7 4.9 copy-start.16
  602.8 17.1 %collective-permute-start.3 = (bf16[1024,512]{1,0:T(8,128)(2,1)S(1)}, bf16[1024,512]{1,0:T(8,128)(2,1)S(1)}, u32[]{:S(2)}, u32[]{:S(2)}) collective-permute-start(bf16[1024,512]{1,0:T(8,128)(2,1)S(1)} %get-tuple-element.353), channel_id=1, source_target_pairs={{0,2},{2,4},{4,6},{6,8},{8,10},{10,12},{12,14},{14,16},{16,18},{18... | collective-permute-start | bytes 3145736 | tf_op jit(solution)/shard_map/ppermute | solution.py:32
  602.9 7.2 copy-start.12
  602.9 17.0 %collective-permute-start.2 = (bf16[1024,512]{1,0:T(8,128)(2,1)S(1)}, bf16[1024,512]{1,0:T(8,128)(2,1)S(1)}, u32[]{:S(2)}, u32[]{:S(2)}) collective-permute-start(bf16[1024,512]{1,0:T(8,128)(2,1)S(1)} %get-tuple-element.352), channel_id=1, source_target_pairs={{0,30},{2,0},{4,2},{6,4},{8,6},{10,8},{12,10},{14,12},{16,14},{18,... | collective-permute-start | bytes 3145736 | tf_op jit(solution)/shard_map/ppermute | solution.py:32
  610.1 9.8 %copy-start.23 = (bf16[512,256]{1,0:T(8,128)(2,1)S(1)}, bf16[512,256]{1,0:T(8,128)(2,1)}, u32[]{:S(2)}) copy-start(bf16[512,256]{1,0:T(8,128)(2,1)} %param.27) | copy-start | bytes 786436
  623.0 71.7 %copy-start.14 = (bf16[1024,512]{1,0:T(8,128)(2,1)S(1)}, bf16[1024,512]{1,0:T(8,128)(2,1)}, u32[]{:S(2)}) copy-start(bf16[1024,512]{1,0:T(8,128)(2,1)} %copy-done.13) | copy-start | bytes 3145732
  623.0 71.7 %copy-start.27 = (f32[1024]{0:T(1024)S(1)}, f32[1024]{0:T(1024)}, u32[]{:S(2)}) copy-start(f32[1024]{0:T(1024)} %copy-done.26) | copy-start | bytes 12292
  623.0 71.7 %copy-start.31 = (f32[512]{0:T(512)S(1)}, f32[512]{0:T(512)}, u32[]{:S(2)}) copy-start(f32[512]{0:T(512)} %param.26) | copy-start | bytes 6148
  694.7 4.0 copy-start.8
  704.9 7.2 copy-start.1
  (76 other events, 149.6 us)
Sparse Core Ops, SparseCore 0:
  204.5 38.8 all-gather.2
  259.9 40.0 all-reduce.3
  623.1 71.5 all-reduce.5
